TPU v7x, 32 devices: a whole 2x2x4 slice. The times are simulated.
32 devices in a mesh: groups: 2 (over y), frames: 4 (over x, core), bands: 4 (over z).
Axes of the slice: x: 2, y: 2, z: 4, core: 2. Of those that a mesh axis runs over, the one named last changes fastest.
Arguments:
- span_tokens: bfloat16 [8, 64, 3072], P(('groups', 'frames')), parts along dimension 0, may hold values from -6 to 6
- w_query: bfloat16 [3072, 3072], P(None, 'bands'), may hold values from -0.109375 to 0.109375
- w_key: bfloat16 [3072, 3072], P(None, 'bands'), may hold values from -0.109375 to 0.109375
- w_value: bfloat16 [3072, 3072], P(None, 'bands'), may hold values from -0.109375 to 0.109375
- cache_keys: bfloat16 [128, 64, 3072], P(('groups', 'frames'), None, 'bands'), parts along dimension 0
- cache_values: bfloat16 [128, 64, 3072], P(('groups', 'frames'), None, 'bands'), parts along dimension 0, may hold values from -6 to 6
- frame_counts: int32 [128], P(('groups', 'frames')), parts along dimension 0, may hold values from 8 to 64, as said below
- rollback_start: int32 [2], P('groups'), parts along dimension 0, may hold values from 32 to 64
- w_proj: bfloat16 [3072, 128], P('bands'), may hold values from -0.109375 to 0.109375
- norm_gain: float32 [128], replicated, may hold values from 0.5 to 2
- conv_first: bfloat16 [3, 3, 3, 128, 128], replicated, may hold values from -0.109375 to 0.109375
- bias_first: float32 [128], replicated, may hold values from -3 to 3
- conv_second: bfloat16 [3, 3, 3, 128, 128], replicated, may hold values from -0.109375 to 0.109375
- bias_second: float32 [128], replicated, may hold values from -3 to 3
Outputs:
- decoded: bfloat16 [8, 16, 16, 128], P(('groups', 'frames'), 'bands'), parts along dimension 0
There are 2 independent parts, one for each index of `groups`. A program takes and returns all parts, laid end to end along the dimension named above; an argument that names none is the same for every part. Nothing has to cross between parts.
Inputs may be any that keep to these rules, and one draw needn't show every extreme that they name: `frame_counts`: some frame has exactly 64 valid tokens and some exactly max(8, 1).
All inputs are finite; a program needn't handle non-finite values.
Results may differ from a plain program's by a relative error of at most 0.014.
Values may be sent and summed in bfloat16 or wider, within the bound.
A program may use at most 128 MiB of HBM per device.

v0:
```python
import functools
import math

import jax
import jax.numpy as jnp
from jax import lax
from jax.experimental import pallas as pl
from jax.experimental.pallas import tpu as pltpu
from jax.sharding import PartitionSpec as P

HD = 128
WT = 8
AGES = 5
MESH = pl.DeviceIdType.MESH
F32 = jnp.float32
BF16 = jnp.bfloat16
NEG = -1e30


def rolled(x, steps):
    rows = x.shape[0]
    column = lax.broadcasted_iota(jnp.int32, x.shape, 0) % WT
    edge = 0 if steps == 1 else WT - 1
    return jnp.where(column == edge, 0.0, pltpu.roll(x, steps % rows, 0))


def kernel(
    frames_n,
    bands_n,
    counts_ref,
    start_ref,
    tokens_hbm,
    wq_hbm,
    wk_hbm,
    wv_hbm,
    keys_hbm,
    values_hbm,
    proj_hbm,
    gain_ref,
    conv1_hbm,
    bias1_ref,
    conv2_hbm,
    bias2_ref,
    out_ref,
    tok,
    wq,
    wk,
    wv,
    kbuf,
    vbuf,
    proj,
    conv1,
    conv2,
    qall,
    pbuf,
    obuf,
    stats,
    part,
    rsbuf,
    lat,
    outf,
    in_sem,
    q_send,
    q_recv,
    pass_send,
    pass_recv,
    chain,
    st_send,
    st_recv,
    rs_send,
    rs_recv,
    ag_send,
    ag_recv,
):
    f = lax.axis_index("frames")
    b = lax.axis_index("bands")
    group_n = frames_n * bands_n
    me = f * bands_n + b
    slot_n = tok.shape[0]
    chunk_n, _, cw = wq.shape
    cached_n = counts_ref.shape[0]
    cached_rows = cached_n * slot_n
    heads = chunk_n * cw // HD
    q_total = frames_n * slot_n
    part_rows = slot_n // bands_n
    band_rows = part_rows // WT
    reach = 2 // band_rows

    sem_i = [0]
    loads = {}

    def load(name, src, dst):
        copy = pltpu.make_async_copy(src, dst, in_sem.at[sem_i[0]])
        sem_i[0] += 1
        copy.start()
        loads[name] = copy

    load("tok", tokens_hbm, tok)
    for c in range(chunk_n):
        load(("q", c), wq_hbm.at[:, pl.ds(c * cw, cw)], wq.at[c])
    load("keys", keys_hbm, kbuf.at[pl.ds(0, cached_rows)])
    for c in range(chunk_n):
        load(("k", c), wk_hbm.at[:, pl.ds(c * cw, cw)], wk.at[c])
    for c in range(chunk_n):
        load(("v", c), wv_hbm.at[:, pl.ds(c * cw, cw)], wv.at[c])
    load("values", values_hbm, vbuf.at[pl.ds(0, cached_rows)])
    load("proj", proj_hbm, proj)
    load("conv1", conv1_hbm, conv1)
    load("conv2", conv2_hbm, conv2)

    lat[...] = jnp.zeros_like(lat)
    barrier = pltpu.get_barrier_semaphore()

    def greet(i, carry):
        pl.semaphore_signal(
            barrier,
            inc=1,
            device_id={"frames": lax.rem(f + i, frames_n)},
            device_id_type=MESH,
        )
        return carry

    lax.fori_loop(1, frames_n, greet, 0)

    def beside(sem, step):
        pl.semaphore_signal(sem, inc=1, device_id={"bands": b + step}, device_id_type=MESH)

    @pl.when(b > 0)
    def _():
        beside(barrier, -1)

    @pl.when(b < bands_n - 1)
    def _():
        beside(barrier, 1)

    greeted = frames_n - 1 + (b > 0).astype(jnp.int32) + (b < bands_n - 1).astype(jnp.int32)

    def relay_entry(step):
        if step > 0:

            @pl.when(b == step)
            def _():
                pl.semaphore_wait(chain.at[0], 1)

            @pl.when(b == bands_n - 1 - step)
            def _():
                pl.semaphore_wait(chain.at[1], 1)

        if step < bands_n - 1:

            @pl.when(b == step)
            def _():
                beside(chain.at[0], 1)

            @pl.when(b == bands_n - 1 - step)
            def _():
                beside(chain.at[1], -1)

    pad_rows = kbuf.shape[0] - cached_rows - slot_n
    kbuf[pl.ds(cached_rows + slot_n, pad_rows), :] = jnp.zeros((pad_rows, kbuf.shape[1]), BF16)
    vbuf[pl.ds(cached_rows + slot_n, pad_rows), :] = jnp.zeros((pad_rows, kbuf.shape[1]), BF16)

    pending = []

    share = 2 if frames_n % 2 == 0 else 1
    core = lax.rem(f, share)
    node = f // share
    nodes = frames_n // share
    mate = f + 1 - 2 * core if share == 2 else f

    def remote(src, dst, send, recv, target, begin=True):
        copy = pltpu.make_async_remote_copy(
            src_ref=src,
            dst_ref=dst,
            send_sem=send,
            recv_sem=recv,
            device_id={"frames": target},
            device_id_type=MESH,
        )
        if begin:
            copy.start()
            pending.append(copy)
        return copy

    def query_copy(c, d, begin):
        step = d if begin else nodes - d
        target = lax.rem(node + step, nodes) * share + core if d > 0 else mate
        rows = qall.at[c, f if begin else target]
        return remote(rows, rows, q_send.at[c, d], q_recv.at[c, d], target, begin)

    def pass_copy(c, d, begin):
        source = lax.rem(node + nodes - d, nodes) * share
        rows = qall.at[c, source + (core if begin else 1 - core)]
        return remote(rows, rows, pass_send.at[c, d], pass_recv.at[c, d], mate, begin)

    first = 0 if share == 2 else 1
    loads["tok"].wait()
    scale = HD ** (-0.5) * math.log2(math.e)
    for c in range(chunk_n):
        loads[("q", c)].wait()
        queries = jnp.dot(tok[...], wq[c], preferred_element_type=F32) * scale
        qall[c, f] = queries.astype(BF16)
        if c == 0:
            pl.semaphore_wait(barrier, greeted)
        for d in [*range(1, nodes), *range(first, 1)]:
            query_copy(c, d, True)
    relay_entry(0)
    for c in range(chunk_n):
        loads[("k", c)].wait()
        kbuf[pl.ds(cached_rows, slot_n), pl.ds(c * cw, cw)] = jnp.dot(
            tok[...], wk[c], preferred_element_type=F32
        ).astype(BF16)
    if bands_n > 1:
        relay_entry(1)
    for c in range(chunk_n):
        loads[("v", c)].wait()
        vbuf[pl.ds(cached_rows, slot_n), pl.ds(c * cw, cw)] = jnp.dot(
            tok[...], wv[c], preferred_element_type=F32
        ).astype(BF16)
        for d in range(1, nodes):
            query_copy(c, d, False).wait_recv()
            if share == 2:
                pass_copy(c, d, True)
    if bands_n > 2:
        relay_entry(2)

    lane = lax.broadcasted_iota(jnp.int32, (1, HD), 1)
    per_tile = HD // slot_n
    bias_tiles = []
    for tile in range(cached_rows // HD):
        visible = lane < 0
        for s in range(per_tile):
            g = tile * per_tile + s
            slot = lane - s * slot_n
            shown = (slot >= 0) & (slot < counts_ref[g]) & (slot < slot_n)
            visible = visible | (shown & ((lane * 0 + (f * cached_n + g)) < start_ref[0]))
        bias_tiles.append(jnp.where(visible, 0.0, NEG))
    bias_row = jnp.concatenate(bias_tiles, 1)

    q_block = min(q_total, 256)
    row = lax.broadcasted_iota(jnp.int32, (q_block, HD), 0)
    wide_lane = lax.broadcasted_iota(jnp.int32, (q_block, HD), 1)

    loads["keys"].wait()
    loads["values"].wait()
    def settle(c):
        if share == 2:
            query_copy(c, 0, False).wait_recv()
            for d in range(1, nodes):
                pass_copy(c, d, False).wait_recv()

    def weigh(h, block):
        per = q_block // slot_n
        q = qall[h * HD // cw, pl.ds(block * per, per), :, pl.ds(h * HD % cw, HD)]
        q = q.reshape(q_block, HD)
        k = kbuf[:, pl.ds(h * HD, HD)]
        raw = lax.dot_general(q, k, (((1,), (1,)), ((), ())), preferred_element_type=F32)
        old = raw[:, :cached_rows] + bias_row
        new = jnp.where(
            (wide_lane < slot_n) & (row + block * q_block >= f * slot_n),
            raw[:, cached_rows:],
            NEG,
        )
        top = jnp.maximum(jnp.max(old, 1, keepdims=True), jnp.max(new, 1, keepdims=True))
        w_old = jnp.exp2(old - top)
        w_new = jnp.exp2(new - top)
        total = jnp.sum(w_old, 1, keepdims=True) + jnp.sum(w_new, 1, keepdims=True)
        pbuf[h, pl.ds(block * q_block, q_block), pl.ds(0, cached_rows)] = w_old.astype(BF16)
        pbuf[h, pl.ds(block * q_block, q_block), pl.ds(cached_rows, HD)] = w_new.astype(BF16)
        return top, total

    def gather(h, block):
        rows = pl.ds(block * q_block, q_block)
        obuf[h, rows, :] = jnp.dot(
            pbuf[h, rows, :], vbuf[:, pl.ds(h * HD, HD)], preferred_element_type=F32
        )

    blocks = range(q_total // q_block)
    late = 2
    for block in blocks:
        stat = jnp.zeros((q_block, HD), F32)
        for h in range(heads):
            if block == 0 and h * HD % cw == 0:
                settle(h * HD // cw)
            top, total = weigh(h, block)
            stat = jnp.where(wide_lane == h, top, stat)
            stat = jnp.where(wide_lane == 8 + h, total, stat)
            if h < heads - late:
                gather(h, block)
        stats[f, :, pl.ds(block * q_block, q_block)] = jnp.transpose(stat)[:16]
    for step in range(3, bands_n):
        relay_entry(step)
    for d in range(1, frames_n):
        copy = pltpu.make_async_remote_copy(
            src_ref=stats.at[f],
            dst_ref=stats.at[f],
            send_sem=st_send.at[d],
            recv_sem=st_recv.at[d],
            device_id={"frames": lax.rem(f + d, frames_n)},
            device_id_type=MESH,
        )
        copy.start()
        pending.append(copy)
    for block in blocks:
        for h in range(heads - late, heads):
            gather(h, block)
    for d in range(1, frames_n):
        source = lax.rem(f + frames_n - d, frames_n)
        pltpu.make_async_remote_copy(
            src_ref=stats.at[source],
            dst_ref=stats.at[source],
            send_sem=st_send.at[d],
            recv_sem=st_recv.at[d],
            device_id={"frames": source},
            device_id_type=MESH,
        ).wait_recv()
    loads["proj"].wait()
    top = stats[0, :8]
    for k in range(1, frames_n):
        top = jnp.maximum(top, stats[k, :8])
    summed = jnp.zeros_like(top)
    for k in range(frames_n):
        summed += jnp.exp2(stats[k, :8] - top) * stats[k, 8:16]
    head_row = lax.broadcasted_iota(jnp.int32, top.shape, 0)
    factor = jnp.where(head_row < heads, jnp.exp2(stats[f, :8] - top) / summed, 0.0)
    factor = jnp.concatenate([factor, jnp.zeros((HD - 8, q_total), F32)], 0)
    for block in blocks:
        rows = pl.ds(block * q_block, q_block)
        column = jnp.transpose(factor[:, block * q_block : (block + 1) * q_block])
        scaled = jnp.concatenate(
            [(obuf[h, rows, :] * column[:, h : h + 1]).astype(BF16) for h in range(heads)], 1
        )
        partial = jnp.dot(scaled, proj[...], preferred_element_type=F32).astype(BF16)
        per = q_block // part_rows
        part[pl.ds(block * per, per)] = partial.reshape(per, part_rows, HD)

    def scatter(i, carry):
        other = lax.rem(me + i, group_n)
        pltpu.make_async_remote_copy(
            src_ref=part.at[other],
            dst_ref=rsbuf.at[me],
            send_sem=rs_send.at[i],
            recv_sem=rs_recv.at[i],
            device_id={"frames": other // bands_n, "bands": lax.rem(other, bands_n)},
            device_id_type=MESH,
        ).start()
        return carry

    lax.fori_loop(1, group_n, scatter, 0)
    rsbuf[me] = part[me]
    loads["conv1"].wait()
    loads["conv2"].wait()

    def received(i, carry):
        other = lax.rem(me + group_n - i, group_n)
        copy = pltpu.make_async_remote_copy(
            src_ref=part.at[other],
            dst_ref=rsbuf.at[other],
            send_sem=rs_send.at[i],
            recv_sem=rs_recv.at[i],
            device_id={"frames": other // bands_n, "bands": lax.rem(other, bands_n)},
            device_id_type=MESH,
        )
        copy.wait_recv()
        return carry

    lax.fori_loop(1, group_n, received, 0)
    own = jnp.sum(rsbuf[...].astype(F32), 0)
    lat[AGES - 1, reach] = own.astype(BF16)

    offsets = [
        (age, e)
        for age in range(min(AGES, frames_n))
        for e in range(-reach, reach + 1)
        if (age, e) != (0, 0)
    ]

    def hand(age, e):
        return pltpu.make_async_remote_copy(
            src_ref=lat.at[AGES - 1, reach],
            dst_ref=lat.at[AGES - 1 - age, reach - e],
            send_sem=ag_send.at[age, e + reach],
            recv_sem=ag_recv.at[age, e + reach],
            device_id={
                "frames": lax.rem(f + age, frames_n),
                "bands": lax.rem(b + e + bands_n, bands_n),
            },
            device_id_type=MESH,
        )

    def sends(age, e):
        return (f + age < frames_n) & (b + e >= 0) & (b + e < bands_n)

    def takes(age, e):
        return (f - age >= 0) & (b - e >= 0) & (b - e < bands_n)

    for age, e in offsets:

        @pl.when(sends(age, e))
        def _(age=age, e=e):
            hand(age, e).start()

    for age, e in offsets:

        @pl.when(takes(age, e))
        def _(age=age, e=e):
            hand(age, e).wait_recv()

    rows_in = band_rows + 4
    rows_mid = band_rows + 2
    latent = lat[...].astype(F32).reshape(AGES, rows_in, WT, HD)
    flat = latent.reshape(AGES * rows_in * WT, HD)
    mean_square = jnp.mean(flat * flat, -1, keepdims=True)
    normed = flat * lax.rsqrt(mean_square + 1e-06) * gain_ref[...]
    active = (normed * jax.nn.sigmoid(normed)).astype(BF16).astype(F32)
    taps = jnp.concatenate([rolled(active, 1), active, rolled(active, -1)], 1)
    taps = taps.reshape(AGES, rows_in, WT, 3 * HD)
    mid = 3 * rows_mid * WT
    acc = jnp.zeros((mid, HD), F32)
    for i in range(3):
        for j in range(3):
            window = taps[i : i + 3, j : j + rows_mid].reshape(mid, 3 * HD).astype(BF16)
            acc += jnp.dot(window, conv1[i * 3 + j], preferred_element_type=F32)
    centre = latent[2:, 1 : 1 + rows_mid].reshape(mid, HD)
    index = lax.broadcasted_iota(jnp.int32, (mid, HD), 0)
    at_frame = index // (rows_mid * WT) + f - 2
    at_row = index // WT % rows_mid + b * band_rows - 1
    inside = (at_frame >= 0) & (at_row >= 0) & (at_row < bands_n * band_rows)
    hidden = jnp.where(inside, centre + (acc + bias1_ref[...]), 0.0).astype(BF16).astype(F32)
    left, right = rolled(hidden, 1), rolled(hidden, -1)
    sides = [
        jnp.concatenate(list(cols), 1).reshape(3, rows_mid, WT, 3 * HD)
        for cols in ((left, hidden, hidden), (hidden, hidden, right))
    ]
    out_rows = 2 * band_rows
    acc = jnp.zeros((2 * out_rows * WT, HD), F32)
    for i in range(3):
        for j in range(3):
            window = jnp.concatenate(
                [side[i, (y + j + 1) // 2] for side in sides for y in range(out_rows)], 0
            ).astype(BF16)
            acc += jnp.dot(window, conv2[i * 3 + j], preferred_element_type=F32)
    acc = acc + bias2_ref[...]
    for p in range(2):
        for y in range(out_rows):
            first = (p * out_rows + y) * WT
            outf[y, pl.ds(p, WT, 2), :] = acc[first : first + WT]
    out_ref[0] = outf[...].astype(BF16)

    for copy in pending:
        copy.wait_send()

    def sent(i, carry):
        pltpu.make_async_remote_copy(
            src_ref=part.at[lax.rem(me + i, group_n)],
            dst_ref=rsbuf.at[me],
            send_sem=rs_send.at[i],
            recv_sem=rs_recv.at[i],
            device_id={"frames": f, "bands": b},
            device_id_type=MESH,
        ).wait_send()
        return carry

    lax.fori_loop(1, group_n, sent, 0)
    for age, e in offsets:

        @pl.when(sends(age, e))
        def _(age=age, e=e):
            hand(age, e).wait_send()


def local(
    frames_n,
    bands_n,
    span_tokens,
    w_query,
    w_key,
    w_value,
    cache_keys,
    cache_values,
    frame_counts,
    rollback_start,
    w_proj,
    norm_gain,
    conv_first,
    bias_first,
    conv_second,
    bias_second,
):
    _, slot_n, width = span_tokens.shape
    cached_n, _, lw = cache_keys.shape
    rows = cached_n * slot_n
    cw = 256 if lw % 256 == 0 else 128
    chunk_n = lw // cw
    heads = lw // HD
    q_total = frames_n * slot_n
    part_rows = slot_n // bands_n
    band_rows = part_rows // WT
    reach = 2 // band_rows
    key_rows = rows + HD
    group_n = frames_n * bands_n
    anywhere = pl.BlockSpec(memory_space=pl.ANY)
    smem = pl.BlockSpec(memory_space=pltpu.SMEM)
    vmem = pl.BlockSpec(memory_space=pltpu.VMEM)
    dma = pltpu.SemaphoreType.DMA
    return pl.pallas_call(
        functools.partial(kernel, frames_n, bands_n),
        out_shape=jax.ShapeDtypeStruct((1, 2 * band_rows, 2 * WT, HD), BF16),
        in_specs=[smem, smem] + [anywhere] * 7 + [vmem, anywhere, vmem, anywhere, vmem],
        out_specs=vmem,
        scratch_shapes=[
            pltpu.VMEM((slot_n, width), BF16),
            pltpu.VMEM((chunk_n, width, cw), BF16),
            pltpu.VMEM((chunk_n, width, cw), BF16),
            pltpu.VMEM((chunk_n, width, cw), BF16),
            pltpu.VMEM((key_rows, lw), BF16),
            pltpu.VMEM((key_rows, lw), BF16),
            pltpu.VMEM((lw, HD), BF16),
            pltpu.VMEM((9, 3 * HD, HD), BF16),
            pltpu.VMEM((9, 3 * HD, HD), BF16),
            pltpu.VMEM((chunk_n, frames_n, slot_n, cw), BF16),
            pltpu.VMEM((heads, q_total, key_rows), BF16),
            pltpu.VMEM((heads, q_total, HD), F32),
            pltpu.VMEM((frames_n, 16, q_total), F32),
            pltpu.VMEM((group_n, part_rows, HD), BF16),
            pltpu.VMEM((group_n, part_rows, HD), BF16),
            pltpu.VMEM((AGES, 2 * reach + 1, part_rows, HD), BF16),
            pltpu.VMEM((2 * band_rows, 2 * WT, HD), F32),
            dma((6 + 3 * chunk_n,)),
            dma((chunk_n, frames_n)),
            dma((chunk_n, frames_n)),
            dma((chunk_n, frames_n)),
            dma((chunk_n, frames_n)),
            pltpu.SemaphoreType.REGULAR((2,)),
            dma((frames_n,)),
            dma((frames_n,)),
            dma((group_n,)),
            dma((group_n,)),
            dma((AGES, 2 * reach + 1)),
            dma((AGES, 2 * reach + 1)),
        ],
        compiler_params=pltpu.CompilerParams(
            collective_id=0, has_side_effects=True, vmem_limit_bytes=60 * 1024 * 1024
        ),
    )(
        frame_counts,
        rollback_start,
        span_tokens.reshape(slot_n, width),
        w_query,
        w_key,
        w_value,
        cache_keys.reshape(rows, lw),
        cache_values.reshape(rows, lw),
        w_proj,
        norm_gain.reshape(1, HD),
        conv_first.reshape(9, 3 * HD, HD),
        bias_first.reshape(1, HD),
        conv_second.reshape(9, 3 * HD, HD),
        bias_second.reshape(1, HD),
    )


def solution(mesh):
    placed = (
        P(("groups", "frames"), None, None),
        P(None, "bands"),
        P(None, "bands"),
        P(None, "bands"),
        P(("groups", "frames"), None, "bands"),
        P(("groups", "frames"), None, "bands"),
        P(("groups", "frames")),
        P("groups"),
        P("bands", None),
        P(),
        P(),
        P(),
        P(),
        P(),
    )
    return jax.shard_map(
        functools.partial(local, mesh.shape["frames"], mesh.shape["bands"]),
        mesh=mesh,
        in_specs=placed,
        out_specs=P(("groups", "frames"), "bands", None, None),
        check_vma=False,
    )
```

profile of v0, /device:TPU:0, one launch (start us, length us, event | category | flops | bytes accessed | tf_op | source)
XLA Modules:
  0.0 29.2 jit_solution(11246063437715586528)
XLA Ops:
  0.7 27.2 %shard_map.136 = bf16[1,4,16,128]{3,2,1,0:T(8,128)(2,1)} custom-call(s32[16]{0:T(128)} %counts_ref.1, s32[1]{0:T(128)S(6)} %copy.16.start_ref, bf16[64,3072]{1,0:T(8,128)(2,1)} %bitcast.12, bf16[3072,768]{1,0:T(8,128)(2,1)} %wq_hbm.1, bf16[3072,768]{1,0:T(8,128)(2,1)} %wk_hbm.1, bf16[3072,768]{1,0:T(8,128)(2,1)} %wv_hbm.1, bf16[1024,768]{1,0:T(8,128)(2,1)} %bitcast.8, ...), custom_call_target="tpu_custom_call" | custom-call | tf_op jit(solution)/shard_map/pallas_call | solution.py:506
  27.9 1.3 %copy.17 = bf16[1,4,16,128]{3,2,1,0:T(8,128)(2,1)} copy(bf16[1,4,16,128]{3,2,1,0:T(8,128)(2,1)} %shard_map.136) | data formatting | bytes 32768
where the time goes:
time: 29.5 us; the launch traced here: 29.2 us
  Pallas kernels  27.2 us (92%)
  local copies, waits for them, and re-layouts  1.32 us (4%)
  between operations  0.66 us (2%)
    pallas_call x1, Pallas kernels, local(): pl.pallas_call(functools.partial(kernel, frames_n, bands_n), out_shape=ja...  27.2 us
    unnamed x1, local copies, waits for them, and re-layouts  1.32 us

commit v1 on v0

v1 whole, which is shorter than its diff:
```python
import functools
import math

import jax
import jax.numpy as jnp
from jax import lax
from jax.experimental import pallas as pl
from jax.experimental.pallas import tpu as pltpu
from jax.sharding import PartitionSpec as P

HD = 128
WT = 8
AGES = 5
LATE = 2
MESH = pl.DeviceIdType.MESH
F32 = jnp.float32
BF16 = jnp.bfloat16
NEG = -1e30


def rolled(x, steps):
    rows = x.shape[0]
    column = lax.broadcasted_iota(jnp.int32, x.shape, 0) % WT
    edge = 0 if steps == 1 else WT - 1
    return jnp.where(column == edge, 0.0, pltpu.roll(x, steps % rows, 0))


def kernel(
    frames_n,
    bands_n,
    counts_ref,
    start_ref,
    tokens_hbm,
    wq_hbm,
    wk_hbm,
    wv_hbm,
    keys_hbm,
    values_hbm,
    proj_hbm,
    gain_ref,
    conv1_hbm,
    bias1_ref,
    conv2_hbm,
    bias2_ref,
    out_ref,
    tok,
    wq,
    wk,
    wv,
    kbuf,
    vbuf,
    proj,
    conv1,
    conv2,
    qall,
    pbuf,
    obuf,
    rbuf,
    st_out,
    st_in,
    colbuf,
    part,
    ybuf,
    outf,
    in_sem,
    q_send,
    q_recv,
    o_send,
    o_recv,
    chain,
    st_send,
    st_recv,
    y_send,
    y_recv,
):
    f = lax.axis_index("frames")
    b = lax.axis_index("bands")
    slot_n = tok.shape[0]
    chunk_n, _, cw = wq.shape
    cached_n = counts_ref.shape[0]
    cached_rows = cached_n * slot_n
    heads = chunk_n * cw // HD
    part_rows = slot_n // bands_n
    band_rows = part_rows // WT
    reach = 2 // band_rows

    sem_i = [0]
    loads = {}

    def load(name, src, dst):
        copy = pltpu.make_async_copy(src, dst, in_sem.at[sem_i[0]])
        sem_i[0] += 1
        copy.start()
        loads[name] = copy

    load("tok", tokens_hbm, tok)
    for c in range(chunk_n):
        load(("q", c), wq_hbm.at[:, pl.ds(c * cw, cw)], wq.at[c])
    for c in range(chunk_n):
        load(("k", c), wk_hbm.at[:, pl.ds(c * cw, cw)], wk.at[c])
    load("keys", keys_hbm, kbuf.at[pl.ds(0, cached_rows)])
    for c in range(chunk_n):
        load(("v", c), wv_hbm.at[:, pl.ds(c * cw, cw)], wv.at[c])
    load("values", values_hbm, vbuf.at[pl.ds(0, cached_rows)])
    load("proj", proj_hbm, proj)
    load("conv1", conv1_hbm, conv1)
    load("conv2", conv2_hbm, conv2)

    ybuf[...] = jnp.zeros_like(ybuf)
    barrier = pltpu.get_barrier_semaphore()

    def greet(i, carry):
        pl.semaphore_signal(
            barrier,
            inc=1,
            device_id={"frames": lax.rem(f + i, frames_n)},
            device_id_type=MESH,
        )
        return carry

    lax.fori_loop(1, frames_n, greet, 0)

    def beside(sem, step):
        pl.semaphore_signal(sem, inc=1, device_id={"bands": b + step}, device_id_type=MESH)

    @pl.when(b > 0)
    def _():
        beside(barrier, -1)

    @pl.when(b < bands_n - 1)
    def _():
        beside(barrier, 1)

    greeted = frames_n - 1 + (b > 0).astype(jnp.int32) + (b < bands_n - 1).astype(jnp.int32)

    def relay_entry(step):
        if step > 0:

            @pl.when(b == step)
            def _():
                pl.semaphore_wait(chain.at[0], 1)

            @pl.when(b == bands_n - 1 - step)
            def _():
                pl.semaphore_wait(chain.at[1], 1)

        if step < bands_n - 1:

            @pl.when(b == step)
            def _():
                beside(chain.at[0], 1)

            @pl.when(b == bands_n - 1 - step)
            def _():
                beside(chain.at[1], -1)

    pad_rows = kbuf.shape[0] - cached_rows - slot_n
    kbuf[pl.ds(cached_rows + slot_n, pad_rows), :] = jnp.zeros((pad_rows, kbuf.shape[1]), BF16)
    vbuf[pl.ds(cached_rows + slot_n, pad_rows), :] = jnp.zeros((pad_rows, kbuf.shape[1]), BF16)

    pending = []

    share = 2 if frames_n % 2 == 0 else 1
    core = lax.rem(f, share)
    node = f // share
    nodes = frames_n // share
    q_block = share * slot_n
    others = [(dn, dc) for dn in range(nodes) for dc in range(share) if (dn, dc) != (0, 0)]
    far = [(dn, dc) for dn, dc in others if dn > 0]
    near = [(dn, dc) for dn, dc in others if dn == 0]

    def node_at(dn):
        return lax.rem(node + dn, nodes)

    def peer(dn, dc):
        return node_at(dn) * share + (1 - core if dc else core)

    def source_of(dn, dc):
        return peer(nodes - dn, dc)

    def remote(src, dst, send, recv, target, begin=True):
        copy = pltpu.make_async_remote_copy(
            src_ref=src,
            dst_ref=dst,
            send_sem=send,
            recv_sem=recv,
            device_id={"frames": target},
            device_id_type=MESH,
        )
        if begin:
            copy.start()
            pending.append(copy)
        return copy

    def query_copy(c, way, begin):
        target = peer(*way) if begin else source_of(*way)
        i = way[0] * share + way[1]
        rows = qall.at[c, f if begin else target]
        return remote(rows, rows, q_send.at[c, i], q_recv.at[c, i], target, begin)

    def output_copy(h, way, begin):
        target = peer(*way) if begin else source_of(*way)
        i = way[0] * share + way[1]
        dst = rbuf.at[f if begin else target, h]
        return remote(obuf.at[target, h], dst, o_send.at[i, h], o_recv.at[i, h], target, begin)

    def stats_copy(way, begin):
        target = peer(*way) if begin else source_of(*way)
        i = way[0] * share + way[1]
        src = st_out.at[target // share]
        dst = st_in.at[f if begin else target]
        return remote(src, dst, st_send.at[i], st_recv.at[i], target, begin)

    loads["tok"].wait()
    scale = HD ** (-0.5) * math.log2(math.e)
    for c in range(chunk_n):
        loads[("q", c)].wait()
        queries = jnp.dot(tok[...], wq[c], preferred_element_type=F32) * scale
        qall[c, f] = queries.astype(BF16)
        if c == 0:
            pl.semaphore_wait(barrier, greeted)
        for way in far + near:
            query_copy(c, way, True)
    relay_entry(0)
    for c in range(chunk_n):
        loads[("k", c)].wait()
        kbuf[pl.ds(cached_rows, slot_n), pl.ds(c * cw, cw)] = jnp.dot(
            tok[...], wk[c], preferred_element_type=F32
        ).astype(BF16)
    if bands_n > 1:
        relay_entry(1)
    for c in range(chunk_n):
        loads[("v", c)].wait()
        vbuf[pl.ds(cached_rows, slot_n), pl.ds(c * cw, cw)] = jnp.dot(
            tok[...], wv[c], preferred_element_type=F32
        ).astype(BF16)
    if bands_n > 2:
        relay_entry(2)

    lane = lax.broadcasted_iota(jnp.int32, (1, HD), 1)
    per_tile = HD // slot_n
    bias_tiles = []
    for tile in range(cached_rows // HD):
        visible = lane < 0
        for s in range(per_tile):
            g = tile * per_tile + s
            slot = lane - s * slot_n
            shown = (slot >= 0) & (slot < counts_ref[g]) & (slot < slot_n)
            visible = visible | (shown & ((lane * 0 + (f * cached_n + g)) < start_ref[0]))
        bias_tiles.append(jnp.where(visible, 0.0, NEG))
    bias_row = jnp.concatenate(bias_tiles, 1)

    row = lax.broadcasted_iota(jnp.int32, (q_block, HD), 0)
    wide_lane = lax.broadcasted_iota(jnp.int32, (q_block, HD), 1)

    loads["keys"].wait()
    loads["values"].wait()

    def weigh(h, base):
        q = qall[h * HD // cw, pl.ds(base, share), :, pl.ds(h * HD % cw, HD)]
        q = q.reshape(q_block, HD)
        k = kbuf[:, pl.ds(h * HD, HD)]
        raw = lax.dot_general(q, k, (((1,), (1,)), ((), ())), preferred_element_type=F32)
        old = raw[:, :cached_rows] + bias_row
        new = jnp.where(
            (wide_lane < slot_n) & (row + base * slot_n >= f * slot_n), raw[:, cached_rows:], NEG
        )
        top = jnp.maximum(jnp.max(old, 1, keepdims=True), jnp.max(new, 1, keepdims=True))
        w_old = jnp.exp2(old - top)
        w_new = jnp.exp2(new - top)
        total = jnp.sum(w_old, 1, keepdims=True) + jnp.sum(w_new, 1, keepdims=True)
        pbuf[h, :, pl.ds(0, cached_rows)] = w_old.astype(BF16)
        pbuf[h, :, pl.ds(cached_rows, HD)] = w_new.astype(BF16)
        return top, total

    def gather(h, base):
        out = jnp.dot(pbuf[h], vbuf[:, pl.ds(h * HD, HD)], preferred_element_type=F32)
        obuf[pl.ds(base, share), h] = out.astype(BF16).reshape(share, slot_n, HD)

    late = min(LATE, heads - 1)
    for dn in range(nodes):
        ways = near if dn == 0 else [way for way in far if way[0] == dn]
        block = node_at(dn)
        base = block * share
        stat = jnp.zeros((q_block, HD), F32)
        for h in range(heads):
            if h * HD % cw == 0:
                back = [((nodes - way[0]) % nodes, way[1]) for way in ways]
                for way in back:
                    query_copy(h * HD // cw, way, False).wait_recv()
            top, total = weigh(h, base)
            stat = jnp.where(wide_lane == h, top, stat)
            stat = jnp.where(wide_lane == 8 + h, total, stat)
            if h < heads - late:
                gather(h, base)
                for way in ways:
                    output_copy(h, way, True)
        st_out[block] = jnp.transpose(stat)[:16]
        for way in ways:
            stats_copy(way, True)
        for h in range(heads - late, heads):
            gather(h, base)
            for way in ways:
                output_copy(h, way, True)
        if dn == 0:
            rbuf[f] = obuf[f]
            st_in[f] = st_out[node]
            for step in range(3, bands_n):
                relay_entry(step)

    loads["proj"].wait()
    for way in others:
        stats_copy(way, False).wait_recv()
    top = st_in[0, :8]
    for k in range(1, frames_n):
        top = jnp.maximum(top, st_in[k, :8])
    parts = [jnp.exp2(st_in[k, :8] - top) for k in range(frames_n)]
    summed = jnp.zeros_like(top)
    for k in range(frames_n):
        summed += parts[k] * st_in[k, 8:16]
    head_row = lax.broadcasted_iota(jnp.int32, top.shape, 0)
    inverse = jnp.where(head_row < heads, 1.0 / summed, 0.0)
    factor = [part_k * inverse for part_k in parts]
    if frames_n * 8 < HD:
        factor.append(jnp.zeros((HD - frames_n * 8, q_block), F32))
    colbuf[...] = jnp.transpose(jnp.concatenate(factor, 0))
    column = colbuf[pl.ds(core * slot_n, slot_n), :]
    partial = jnp.zeros((slot_n, HD), F32)
    for c in range(chunk_n):
        attended = []
        for h in range(c * cw // HD, (c + 1) * cw // HD):
            for way in others:
                output_copy(h, way, False).wait_recv()
            mixed = jnp.zeros((slot_n, HD), F32)
            for k in range(frames_n):
                i = k * 8 + h
                mixed += rbuf[k, h].astype(F32) * column[:, i : i + 1]
            attended.append(mixed.astype(BF16))
        partial += jnp.dot(
            jnp.concatenate(attended, 1), proj[pl.ds(c * cw, cw), :], preferred_element_type=F32
        )
    part[...] = partial.astype(BF16).reshape(bands_n, part_rows, HD)

    width = min(2 * reach + 1, bands_n)
    offsets = [
        (age, e)
        for age in range(min(AGES, frames_n))
        for e in range(bands_n)
        if (age, e) != (0, 0)
    ]

    def hand(age, e, begin):
        other = lax.rem(b + (e if begin else bands_n - e), bands_n)
        goal = other if begin else b
        first = jnp.clip(goal - reach, 0, bands_n - width)
        return pltpu.make_async_remote_copy(
            src_ref=part.at[pl.ds(first, width)],
            dst_ref=ybuf.at[AGES - 1 - age, b if begin else other, pl.ds(first + reach, width)],
            send_sem=y_send.at[age, e],
            recv_sem=y_recv.at[age, e],
            device_id={"frames": lax.rem(f + age, frames_n), "bands": other},
            device_id_type=MESH,
        )

    def sends(age):
        return f + age < frames_n

    def takes(age):
        return f - age >= 0

    for age, e in sorted(offsets, key=lambda o: (-o[0], -o[1])):

        @pl.when(sends(age))
        def _(age=age, e=e):
            hand(age, e, True).start()

    ybuf[AGES - 1, b, pl.ds(reach, bands_n)] = part[...]
    loads["conv1"].wait()
    loads["conv2"].wait()
    for age, e in offsets:

        @pl.when(takes(age))
        def _(age=age, e=e):
            hand(age, e, False).wait_recv()

    latent = jnp.zeros((AGES, 2 * reach + 1, part_rows, HD), F32)
    for s in range(bands_n):
        latent += ybuf[:, s, pl.ds(b, 2 * reach + 1)].astype(F32)

    rows_in = band_rows + 4
    rows_mid = band_rows + 2
    latent = latent.astype(BF16).astype(F32).reshape(AGES, rows_in, WT, HD)
    flat = latent.reshape(AGES * rows_in * WT, HD)
    mean_square = jnp.mean(flat * flat, -1, keepdims=True)
    normed = flat * lax.rsqrt(mean_square + 1e-06) * gain_ref[...]
    active = (normed * jax.nn.sigmoid(normed)).astype(BF16).astype(F32)
    taps = jnp.concatenate([rolled(active, 1), active, rolled(active, -1)], 1)
    taps = taps.reshape(AGES, rows_in, WT, 3 * HD)
    mid = 3 * rows_mid * WT
    acc = jnp.zeros((mid, HD), F32)
    for i in range(3):
        for j in range(3):
            window = taps[i : i + 3, j : j + rows_mid].reshape(mid, 3 * HD).astype(BF16)
            acc += jnp.dot(window, conv1[i * 3 + j], preferred_element_type=F32)
    centre = latent[2:, 1 : 1 + rows_mid].reshape(mid, HD)
    index = lax.broadcasted_iota(jnp.int32, (mid, HD), 0)
    at_frame = index // (rows_mid * WT) + f - 2
    at_row = index // WT % rows_mid + b * band_rows - 1
    inside = (at_frame >= 0) & (at_row >= 0) & (at_row < bands_n * band_rows)
    hidden = jnp.where(inside, centre + (acc + bias1_ref[...]), 0.0).astype(BF16).astype(F32)
    left, right = rolled(hidden, 1), rolled(hidden, -1)
    sides = [
        jnp.concatenate(list(cols), 1).reshape(3, rows_mid, WT, 3 * HD)
        for cols in ((left, hidden, hidden), (hidden, hidden, right))
    ]
    out_rows = 2 * band_rows
    acc = jnp.zeros((2 * out_rows * WT, HD), F32)
    for i in range(3):
        for j in range(3):
            window = jnp.concatenate(
                [side[i, (y + j + 1) // 2] for side in sides for y in range(out_rows)], 0
            ).astype(BF16)
            acc += jnp.dot(window, conv2[i * 3 + j], preferred_element_type=F32)
    acc = acc + bias2_ref[...]
    for p in range(2):
        for y in range(out_rows):
            first = (p * out_rows + y) * WT
            outf[y, pl.ds(p, WT, 2), :] = acc[first : first + WT]
    out_ref[0] = outf[...].astype(BF16)

    for copy in pending:
        copy.wait_send()
    for age, e in offsets:

        @pl.when(sends(age))
        def _(age=age, e=e):
            hand(age, e, True).wait_send()


def local(
    frames_n,
    bands_n,
    span_tokens,
    w_query,
    w_key,
    w_value,
    cache_keys,
    cache_values,
    frame_counts,
    rollback_start,
    w_proj,
    norm_gain,
    conv_first,
    bias_first,
    conv_second,
    bias_second,
):
    _, slot_n, width = span_tokens.shape
    cached_n, _, lw = cache_keys.shape
    rows = cached_n * slot_n
    cw = 256 if lw % 256 == 0 else 128
    chunk_n = lw // cw
    heads = lw // HD
    share = 2 if frames_n % 2 == 0 else 1
    q_block = share * slot_n
    part_rows = slot_n // bands_n
    band_rows = part_rows // WT
    reach = 2 // band_rows
    key_rows = rows + HD
    anywhere = pl.BlockSpec(memory_space=pl.ANY)
    smem = pl.BlockSpec(memory_space=pltpu.SMEM)
    vmem = pl.BlockSpec(memory_space=pltpu.VMEM)
    dma = pltpu.SemaphoreType.DMA
    return pl.pallas_call(
        functools.partial(kernel, frames_n, bands_n),
        out_shape=pltpu.VMEM((1, 2 * band_rows, 2 * WT, HD), BF16),
        in_specs=[smem, smem] + [anywhere] * 7 + [vmem, anywhere, vmem, anywhere, vmem],
        out_specs=vmem,
        scratch_shapes=[
            pltpu.VMEM((slot_n, width), BF16),
            pltpu.VMEM((chunk_n, width, cw), BF16),
            pltpu.VMEM((chunk_n, width, cw), BF16),
            pltpu.VMEM((chunk_n, width, cw), BF16),
            pltpu.VMEM((key_rows, lw), BF16),
            pltpu.VMEM((key_rows, lw), BF16),
            pltpu.VMEM((lw, HD), BF16),
            pltpu.VMEM((9, 3 * HD, HD), BF16),
            pltpu.VMEM((9, 3 * HD, HD), BF16),
            pltpu.VMEM((chunk_n, frames_n, slot_n, cw), BF16),
            pltpu.VMEM((heads, q_block, key_rows), BF16),
            pltpu.VMEM((frames_n, heads, slot_n, HD), BF16),
            pltpu.VMEM((frames_n, heads, slot_n, HD), BF16),
            pltpu.VMEM((frames_n // share, 16, q_block), F32),
            pltpu.VMEM((frames_n, 16, q_block), F32),
            pltpu.VMEM((q_block, HD), F32),
            pltpu.VMEM((bands_n, part_rows, HD), BF16),
            pltpu.VMEM((AGES, bands_n, bands_n + 2 * reach, part_rows, HD), BF16),
            pltpu.VMEM((2 * band_rows, 2 * WT, HD), F32),
            dma((6 + 3 * chunk_n,)),
            dma((chunk_n, frames_n)),
            dma((chunk_n, frames_n)),
            dma((frames_n, heads)),
            dma((frames_n, heads)),
            pltpu.SemaphoreType.REGULAR((2,)),
            dma((frames_n,)),
            dma((frames_n,)),
            dma((AGES, bands_n)),
            dma((AGES, bands_n)),
        ],
        compiler_params=pltpu.CompilerParams(
            collective_id=0, has_side_effects=True, vmem_limit_bytes=60 * 1024 * 1024
        ),
    )(
        frame_counts,
        rollback_start,
        span_tokens.reshape(slot_n, width),
        w_query,
        w_key,
        w_value,
        cache_keys.reshape(rows, lw),
        cache_values.reshape(rows, lw),
        w_proj,
        norm_gain.reshape(1, HD),
        conv_first.reshape(9, 3 * HD, HD),
        bias_first.reshape(1, HD),
        conv_second.reshape(9, 3 * HD, HD),
        bias_second.reshape(1, HD),
    )


def solution(mesh):
    placed = (
        P(("groups", "frames"), None, None),
        P(None, "bands"),
        P(None, "bands"),
        P(None, "bands"),
        P(("groups", "frames"), None, "bands"),
        P(("groups", "frames"), None, "bands"),
        P(("groups", "frames")),
        P("groups"),
        P("bands", None),
        P(),
        P(),
        P(),
        P(),
        P(),
    )
    return jax.shard_map(
        functools.partial(local, mesh.shape["frames"], mesh.shape["bands"]),
        mesh=mesh,
        in_specs=placed,
        out_specs=P(("groups", "frames"), "bands", None, None),
        check_vma=False,
    )
```

time: 29.5 us -> 31 us (1.051)
  Pallas kernels: 27.2 us -> 29.6 us
  local copies, waits for them, and re-layouts: 1.32 us -> 0.61 us
    pallas_call x1, Pallas kernels: 27.2 us -> 29.6 us  [local(): pl.pallas_call(functools.partial(kernel, frames_n, bands_n), out_shape=pl...]
    unnamed x1, local copies, waits for them, and re-layouts: 1.32 us -> 0.61 us
where the time goes in v1:
time: 31 us; the launch traced here: 30.8 us
  Pallas kernels  29.6 us (95%)
  between operations  0.66 us (2%)
  local copies, waits for them, and re-layouts  0.61 us (2%)
    pallas_call x1, Pallas kernels, local(): pl.pallas_call(functools.partial(kernel, frames_n, bands_n), out_shape=pl...  29.6 us

profile of v1, /device:TPU:0, one launch (start us, length us, event | category | flops | bytes accessed | tf_op | source)
XLA Modules:
  0.0 30.8 jit_solution(4113699373901915159)
XLA Ops:
  0.7 29.6 %shard_map.136 = bf16[1,4,16,128]{3,2,1,0:T(8,128)(2,1)S(1)} custom-call(s32[16]{0:T(128)} %counts_ref.1, s32[1]{0:T(128)S(6)} %copy.17.start_ref, bf16[64,3072]{1,0:T(8,128)(2,1)} %bitcast.12, bf16[3072,768]{1,0:T(8,128)(2,1)} %wq_hbm.1, bf16[3072,768]{1,0:T(8,128)(2,1)} %wk_hbm.1, bf16[3072,768]{1,0:T(8,128)(2,1)} %wv_hbm.1, bf16[1024,768]{1,0:T(8,128)(2,1)} %bitcast.8, ...), custom_call_target="tpu_custom_call" | custom-call | tf_op jit(solution)/shard_map/pallas_call | solution.py:474
  30.2 0.6 %copy.16 = bf16[1,4,16,128]{3,2,1,0:T(8,128)(2,1)} copy(bf16[1,4,16,128]{3,2,1,0:T(8,128)(2,1)S(1)} %shard_map.136) | data formatting | bytes 32768

commit v2 on v0

--- a/solution.py
+++ b/solution.py
@@ -98,11 +98,11 @@
     load("tok", tokens_hbm, tok)
     for c in range(chunk_n):
         load(("q", c), wq_hbm.at[:, pl.ds(c * cw, cw)], wq.at[c])
-    load("keys", keys_hbm, kbuf.at[pl.ds(0, cached_rows)])
     for c in range(chunk_n):
         load(("k", c), wk_hbm.at[:, pl.ds(c * cw, cw)], wk.at[c])
     for c in range(chunk_n):
         load(("v", c), wv_hbm.at[:, pl.ds(c * cw, cw)], wv.at[c])
+    load("keys", keys_hbm, kbuf.at[pl.ds(0, cached_rows)])
     load("values", values_hbm, vbuf.at[pl.ds(0, cached_rows)])
     load("proj", proj_hbm, proj)
     load("conv1", conv1_hbm, conv1)
@@ -161,12 +161,6 @@
     vbuf[pl.ds(cached_rows + slot_n, pad_rows), :] = jnp.zeros((pad_rows, kbuf.shape[1]), BF16)
 
     pending = []
-
-    share = 2 if frames_n % 2 == 0 else 1
-    core = lax.rem(f, share)
-    node = f // share
-    nodes = frames_n // share
-    mate = f + 1 - 2 * core if share == 2 else f
 
     def remote(src, dst, send, recv, target, begin=True):
         copy = pltpu.make_async_remote_copy(
@@ -182,6 +176,13 @@
             pending.append(copy)
         return copy
 
+    share = 2 if frames_n % 2 == 0 else 1
+    core = lax.rem(f, share)
+    node = f // share
+    nodes = frames_n // share
+    mate = f + 1 - 2 * core if share == 2 else f
+    first = 0 if share == 2 else 1
+
     def query_copy(c, d, begin):
         step = d if begin else nodes - d
         target = lax.rem(node + step, nodes) * share + core if d > 0 else mate
@@ -193,7 +194,12 @@
         rows = qall.at[c, source + (core if begin else 1 - core)]
         return remote(rows, rows, pass_send.at[c, d], pass_recv.at[c, d], mate, begin)
 
-    first = 0 if share == 2 else 1
+    def relay_queries(c):
+        for d in range(1, nodes):
+            query_copy(c, d, False).wait_recv()
+            if share == 2:
+                pass_copy(c, d, True)
+
     loads["tok"].wait()
     scale = HD ** (-0.5) * math.log2(math.e)
     for c in range(chunk_n):
@@ -210,19 +216,14 @@
         kbuf[pl.ds(cached_rows, slot_n), pl.ds(c * cw, cw)] = jnp.dot(
             tok[...], wk[c], preferred_element_type=F32
         ).astype(BF16)
-    if bands_n > 1:
-        relay_entry(1)
     for c in range(chunk_n):
         loads[("v", c)].wait()
         vbuf[pl.ds(cached_rows, slot_n), pl.ds(c * cw, cw)] = jnp.dot(
             tok[...], wv[c], preferred_element_type=F32
         ).astype(BF16)
-        for d in range(1, nodes):
-            query_copy(c, d, False).wait_recv()
-            if share == 2:
-                pass_copy(c, d, True)
-    if bands_n > 2:
-        relay_entry(2)
+        relay_queries(c)
+    if bands_n > 1:
+        relay_entry(1)
 
     lane = lax.broadcasted_iota(jnp.int32, (1, HD), 1)
     per_tile = HD // slot_n
@@ -243,6 +244,7 @@
 
     loads["keys"].wait()
     loads["values"].wait()
+
     def settle(c):
         if share == 2:
             query_copy(c, 0, False).wait_recv()
@@ -276,7 +278,7 @@
         )
 
     blocks = range(q_total // q_block)
-    late = 2
+    late = min(4, heads - 1)
     for block in blocks:
         stat = jnp.zeros((q_block, HD), F32)
         for h in range(heads):
@@ -288,8 +290,8 @@
             if h < heads - late:
                 gather(h, block)
         stats[f, :, pl.ds(block * q_block, q_block)] = jnp.transpose(stat)[:16]
-    for step in range(3, bands_n):
-        relay_entry(step)
+    if bands_n > 2:
+        relay_entry(2)
     for d in range(1, frames_n):
         copy = pltpu.make_async_remote_copy(
             src_ref=stats.at[f],
@@ -314,6 +316,8 @@
             device_id={"frames": source},
             device_id_type=MESH,
         ).wait_recv()
+    for step in range(3, bands_n):
+        relay_entry(step)
     loads["proj"].wait()
     top = stats[0, :8]
     for k in range(1, frames_n):
@@ -346,7 +350,7 @@
         ).start()
         return carry
 
-    lax.fori_loop(1, group_n, scatter, 0)
+    lax.fori_loop(1, group_n, scatter, 0, unroll=group_n <= 16)
     rsbuf[me] = part[me]
     loads["conv1"].wait()
     loads["conv2"].wait()
@@ -364,7 +368,7 @@
         copy.wait_recv()
         return carry
 
-    lax.fori_loop(1, group_n, received, 0)
+    lax.fori_loop(1, group_n, received, 0, unroll=group_n <= 16)
     own = jnp.sum(rsbuf[...].astype(F32), 0)
     lat[AGES - 1, reach] = own.astype(BF16)
 
@@ -461,7 +465,7 @@
         ).wait_send()
         return carry
 
-    lax.fori_loop(1, group_n, sent, 0)
+    lax.fori_loop(1, group_n, sent, 0, unroll=group_n <= 16)
     for age, e in offsets:
 
         @pl.when(sends(age, e))
@@ -505,7 +509,7 @@
     dma = pltpu.SemaphoreType.DMA
     return pl.pallas_call(
         functools.partial(kernel, frames_n, bands_n),
-        out_shape=jax.ShapeDtypeStruct((1, 2 * band_rows, 2 * WT, HD), BF16),
+        out_shape=pltpu.VMEM((1, 2 * band_rows, 2 * WT, HD), BF16),
         in_specs=[smem, smem] + [anywhere] * 7 + [vmem, anywhere, vmem, anywhere, vmem],
         out_specs=vmem,
         scratch_shapes=[

time: 29.5 us -> 27.4 us (0.929)
  Pallas kernels: 27.2 us -> 26 us
  local copies, waits for them, and re-layouts: 1.32 us -> 0.61 us
    pallas_call x1, Pallas kernels: 27.2 us -> 26 us  [local(): pl.pallas_call(functools.partial(kernel, frames_n, bands_n), out_shape=pl...]
    unnamed x1, local copies, waits for them, and re-layouts: 1.32 us -> 0.61 us
where the time goes in v2:
time: 27.4 us; the launch traced here: 27.3 us
  Pallas kernels  26 us (95%)
  between operations  0.66 us (2%)
  local copies, waits for them, and re-layouts  0.61 us (2%)
    pallas_call x1, Pallas kernels, local(): pl.pallas_call(functools.partial(kernel, frames_n, bands_n), out_shape=pl...  26 us
    unnamed x1, local copies, waits for them, and re-layouts  0.61 us

profile of v2, /device:TPU:0, one launch (start us, length us, event | category | flops | bytes accessed | tf_op | source)
XLA Modules:
  0.0 27.3 jit_solution(16204232481516648535)
XLA Ops:
  0.7 26.0 %shard_map.136 = bf16[1,4,16,128]{3,2,1,0:T(8,128)(2,1)S(1)} custom-call(s32[16]{0:T(128)} %counts_ref.1, s32[1]{0:T(128)S(6)} %copy.17.start_ref, bf16[64,3072]{1,0:T(8,128)(2,1)} %bitcast.12, bf16[3072,768]{1,0:T(8,128)(2,1)} %wq_hbm.1, bf16[3072,768]{1,0:T(8,128)(2,1)} %wk_hbm.1, bf16[3072,768]{1,0:T(8,128)(2,1)} %wv_hbm.1, bf16[1024,768]{1,0:T(8,128)(2,1)} %bitcast.8, ...), custom_call_target="tpu_custom_call" | custom-call | tf_op jit(solution)/shard_map/pallas_call | solution.py:510
  26.7 0.6 %copy.16 = bf16[1,4,16,128]{3,2,1,0:T(8,128)(2,1)} copy(bf16[1,4,16,128]{3,2,1,0:T(8,128)(2,1)S(1)} %shard_map.136) | data formatting | bytes 32768

commit v3 on v2

--- a/solution.py
+++ b/solution.py
@@ -278,7 +278,7 @@
         )
 
     blocks = range(q_total // q_block)
-    late = min(4, heads - 1)
+    late = heads
     for block in blocks:
         stat = jnp.zeros((q_block, HD), F32)
         for h in range(heads):

time: 27.4 us -> 27 us (0.985)
  Pallas kernels: 26 us -> 25.6 us
    pallas_call x1, Pallas kernels: 26 us -> 25.6 us  [local(): pl.pallas_call(functools.partial(kernel, frames_n, bands_n), out_shape=pl...]
where the time goes in v3:
time: 27 us; the launch traced here: 26.9 us
  Pallas kernels  25.6 us (95%)
  between operations  0.66 us (2%)
  local copies, waits for them, and re-layouts  0.61 us (2%)
    pallas_call x1, Pallas kernels, local(): pl.pallas_call(functools.partial(kernel, frames_n, bands_n), out_shape=pl...  25.6 us
    unnamed x1, local copies, waits for them, and re-layouts  0.61 us

profile of v3, /device:TPU:0, one launch (start us, length us, event | category | flops | bytes accessed | tf_op | source)
XLA Modules:
  0.0 26.9 jit_solution(1284686476247947562)
XLA Ops:
  0.7 25.6 %shard_map.136 = bf16[1,4,16,128]{3,2,1,0:T(8,128)(2,1)S(1)} custom-call(s32[16]{0:T(128)} %counts_ref.1, s32[1]{0:T(128)S(6)} %copy.17.start_ref, bf16[64,3072]{1,0:T(8,128)(2,1)} %bitcast.12, bf16[3072,768]{1,0:T(8,128)(2,1)} %wq_hbm.1, bf16[3072,768]{1,0:T(8,128)(2,1)} %wk_hbm.1, bf16[3072,768]{1,0:T(8,128)(2,1)} %wv_hbm.1, bf16[1024,768]{1,0:T(8,128)(2,1)} %bitcast.8, ...), custom_call_target="tpu_custom_call" | custom-call | tf_op jit(solution)/shard_map/pallas_call | solution.py:510
  26.2 0.6 %copy.16 = bf16[1,4,16,128]{3,2,1,0:T(8,128)(2,1)} copy(bf16[1,4,16,128]{3,2,1,0:T(8,128)(2,1)S(1)} %shard_map.136) | data formatting | bytes 32768

commit v4 on v3

--- a/solution.py
+++ b/solution.py
@@ -100,9 +100,9 @@
         load(("q", c), wq_hbm.at[:, pl.ds(c * cw, cw)], wq.at[c])
     for c in range(chunk_n):
         load(("k", c), wk_hbm.at[:, pl.ds(c * cw, cw)], wk.at[c])
+    load("keys", keys_hbm, kbuf.at[pl.ds(0, cached_rows)])
     for c in range(chunk_n):
         load(("v", c), wv_hbm.at[:, pl.ds(c * cw, cw)], wv.at[c])
-    load("keys", keys_hbm, kbuf.at[pl.ds(0, cached_rows)])
     load("values", values_hbm, vbuf.at[pl.ds(0, cached_rows)])
     load("proj", proj_hbm, proj)
     load("conv1", conv1_hbm, conv1)
@@ -217,10 +217,6 @@
             tok[...], wk[c], preferred_element_type=F32
         ).astype(BF16)
     for c in range(chunk_n):
-        loads[("v", c)].wait()
-        vbuf[pl.ds(cached_rows, slot_n), pl.ds(c * cw, cw)] = jnp.dot(
-            tok[...], wv[c], preferred_element_type=F32
-        ).astype(BF16)
         relay_queries(c)
     if bands_n > 1:
         relay_entry(1)
@@ -243,7 +239,6 @@
     wide_lane = lax.broadcasted_iota(jnp.int32, (q_block, HD), 1)
 
     loads["keys"].wait()
-    loads["values"].wait()
 
     def settle(c):
         if share == 2:
@@ -303,6 +298,12 @@
         )
         copy.start()
         pending.append(copy)
+    for c in range(chunk_n):
+        loads[("v", c)].wait()
+        vbuf[pl.ds(cached_rows, slot_n), pl.ds(c * cw, cw)] = jnp.dot(
+            tok[...], wv[c], preferred_element_type=F32
+        ).astype(BF16)
+    loads["values"].wait()
     for block in blocks:
         for h in range(heads - late, heads):
             gather(h, block)

time: 27 us -> 26.7 us (0.989)
  Pallas kernels: 25.6 us -> 25.2 us
    pallas_call x1, Pallas kernels: 25.6 us -> 25.2 us  [local(): pl.pallas_call(functools.partial(kernel, frames_n, bands_n), out_shape=pl...]
where the time goes in v4:
time: 26.7 us; the launch traced here: 26.5 us
  Pallas kernels  25.2 us (94%)
  between operations  0.66 us (2%)
  local copies, waits for them, and re-layouts  0.61 us (2%)
    pallas_call x1, Pallas kernels, local(): pl.pallas_call(functools.partial(kernel, frames_n, bands_n), out_shape=pl...  25.2 us
    unnamed x1, local copies, waits for them, and re-layouts  0.61 us

profile of v4, /device:TPU:0, one launch (start us, length us, event | category | flops | bytes accessed | tf_op | source)
XLA Modules:
  0.0 26.5 jit_solution(10439091705622050866)
XLA Ops:
  0.7 25.2 %shard_map.136 = bf16[1,4,16,128]{3,2,1,0:T(8,128)(2,1)S(1)} custom-call(s32[16]{0:T(128)} %counts_ref.1, s32[1]{0:T(128)S(6)} %copy.17.start_ref, bf16[64,3072]{1,0:T(8,128)(2,1)} %bitcast.12, bf16[3072,768]{1,0:T(8,128)(2,1)} %wq_hbm.1, bf16[3072,768]{1,0:T(8,128)(2,1)} %wk_hbm.1, bf16[3072,768]{1,0:T(8,128)(2,1)} %wv_hbm.1, bf16[1024,768]{1,0:T(8,128)(2,1)} %bitcast.8, ...), custom_call_target="tpu_custom_call" | custom-call | tf_op jit(solution)/shard_map/pallas_call | solution.py:511
  25.9 0.6 %copy.16 = bf16[1,4,16,128]{3,2,1,0:T(8,128)(2,1)} copy(bf16[1,4,16,128]{3,2,1,0:T(8,128)(2,1)S(1)} %shard_map.136) | data formatting | bytes 32768
